TPU v7x, 256 devices: a whole 4x4x8 slice. The times are simulated.
256 devices in a mesh: outer: 16 (over z, core), inner: 16 (over y, x).
Axes of the slice: x: 4, y: 4, z: 8, core: 2. Of those that a mesh axis runs over, the one named last changes fastest.
Arguments:
- queries: bfloat16 [32768, 4096], P(('outer', 'inner')), may hold values from -48 to 48
- keys: bfloat16 [32768, 1024], P(('outer', 'inner')), may hold values from -20 to 20
- values: bfloat16 [32768, 1024], P(('outer', 'inner')), may hold values from -6 to 6
- ancestors: int32 [256, 8], replicated, may hold values from -1 to 255, as said below
- token_block: int32 [32768], replicated, may hold values from 0 to 255, as said below
- positions: int32 [32768], replicated, may hold values from 0 to 1023, as said below
Outputs:
- attended: bfloat16 [32768, 4096], P(('outer', 'inner'))
Inputs may be any that keep to these rules, and one draw needn't show every extreme that they name: `ancestors`: row b lists the blocks on the path from the root block 0 to block b, root first and b last, then -1; a parent has a smaller number than its child; some row lists 8 blocks. `token_block`: each aligned span of 128 tokens belongs to one block, and every block fills exactly one span; apart from block 0, no two blocks of one root path lie in the same aligned group of 2048 tokens. `positions`: a token's position is 128 times (the number of blocks on its block's root path minus 1) plus its offset within its span.
All inputs are finite; a program needn't handle non-finite values.
Results may differ from a plain program's by a relative error of at most 0.0065.
Values may be sent and summed in bfloat16 or wider, within the bound.
No kernel may reach another device: no remote copies, remote signals or barrier semaphores. Data moves between devices by JAX's collectives and lax.ppermute only.
A program may use at most 128 MiB of HBM per device.

v0:
```python
import jax
import jax.numpy as jnp
from jax import lax
from jax.sharding import PartitionSpec as P

HEADS = 32
KV_HEADS = 8
HEAD_DIM = 128
BLOCK = 128
ANC_MAX = 8
ROTARY_BASE = 500000.0


def rotate(matrix, places, head_count):
    row_count = matrix.shape[0]
    head_width = matrix.shape[1] // head_count
    half_width = head_width // 2
    inverse = ROTARY_BASE ** (-2.0 * jnp.arange(half_width, dtype=jnp.float32) / head_width)
    angles = places.astype(jnp.float32)[:, None] * inverse[None, :]
    cosine = jnp.cos(angles)[:, None, :]
    sine_part = jnp.sin(angles)[:, None, :]
    unfolded = matrix.astype(jnp.float32).reshape(row_count, head_count, head_width)
    leading = unfolded[:, :, :half_width]
    trailing = unfolded[:, :, half_width:]
    turned = jnp.concatenate(
        [leading * cosine - trailing * sine_part, trailing * cosine + leading * sine_part], axis=2
    )
    return turned.reshape(row_count, head_count * head_width).astype(jnp.bfloat16)


def shards(queries, keys, values, ancestors, token_block, positions):
    tok_rows = queries.shape[0]
    span_count = tok_rows // BLOCK
    group_size = HEADS // KV_HEADS
    kv_width = keys.shape[1]
    outer_count = lax.axis_size("outer")
    inner_count = lax.axis_size("inner")
    outer_me = lax.axis_index("outer")
    inner_me = lax.axis_index("inner")
    device_me = outer_me * inner_count + inner_me
    start_row = device_me * tok_rows
    own_places = lax.dynamic_slice_in_dim(positions, start_row, tok_rows)
    rot_q = rotate(queries, own_places, HEADS)
    rot_k = rotate(keys, own_places, KV_HEADS)
    block_count = ancestors.shape[0]
    block_ids = jnp.arange(block_count, dtype=jnp.int32)
    span_blocks = token_block[::BLOCK]
    span_of = jnp.sum(
        jnp.where(span_blocks[:, None] == block_ids[None, :], block_ids[:, None], 0), axis=0
    )
    group_spans = inner_count * span_count
    capacity = 2
    span_ids = jnp.arange(span_count, dtype=jnp.int32)
    slot_ids = jnp.arange(capacity, dtype=jnp.int32)
    bundled = (
        lax.all_gather(rot_k, "inner", axis=0, tiled=True),
        lax.all_gather(values, "inner", axis=0, tiled=True),
    )
    key_blocks = bundled[0].reshape(group_spans, BLOCK, kv_width)
    value_blocks = bundled[1].reshape(group_spans, BLOCK, kv_width)
    dest_outer = jnp.arange(outer_count, dtype=jnp.int32)
    dest_spans = (dest_outer[:, None] * inner_count + inner_me) * span_count + span_ids[None, :]
    dest_lineage = ancestors[span_blocks[dest_spans]]
    lineage_spans = span_of[jnp.maximum(dest_lineage, 0)]
    counted = dest_lineage >= 0
    matches = counted & (lineage_spans // group_spans == outer_me)
    slot_rank = jnp.cumsum(matches.astype(jnp.int32), axis=2) - 1
    local_spans = lineage_spans - outer_me * group_spans
    picked = jnp.sum(
        jnp.where(
            matches[..., None] & (slot_rank[..., None] == slot_ids), local_spans[..., None], 0
        ),
        axis=2,
    )
    send_keys = key_blocks[picked]
    send_values = value_blocks[picked]
    received = (
        lax.all_to_all(send_keys, "outer", split_axis=0, concat_axis=0, tiled=True),
        lax.all_to_all(send_values, "outer", split_axis=0, concat_axis=0, tiled=True),
    )
    own_spans = device_me * span_count + span_ids
    own_lineage = ancestors[span_blocks[own_spans]]
    own_valid = own_lineage >= 0
    own_span_of = span_of[jnp.maximum(own_lineage, 0)]
    own_groups = own_span_of // group_spans
    path_ids = jnp.arange(ANC_MAX, dtype=jnp.int32)
    earlier = path_ids[None, :] < path_ids[:, None]
    same_group = (
        own_valid[:, None, :]
        & (own_groups[:, :, None] == own_groups[:, None, :])
        & earlier[None, :, :]
    )
    own_rank = jnp.minimum(jnp.sum(same_group.astype(jnp.int32), axis=2), capacity - 1)
    slot_index = (own_groups * span_count + span_ids[:, None]) * capacity + own_rank
    slot_total = outer_count * span_count * capacity
    got_keys = received[0].reshape(slot_total, BLOCK, kv_width)[slot_index]
    got_values = received[1].reshape(slot_total, BLOCK, kv_width)[slot_index]
    offsets = jnp.arange(BLOCK, dtype=jnp.int32)
    key_index = (own_span_of[:, :, None] * BLOCK + offsets[None, None, :]).reshape(
        span_count, ANC_MAX * BLOCK
    )
    key_places = positions[key_index]
    query_places = own_places.reshape(span_count, BLOCK)
    allowed = jnp.repeat(own_valid, BLOCK, axis=1)[:, None, :] & (
        key_places[:, None, :] <= query_places[:, :, None]
    )
    query_rows = rot_q.reshape(span_count, BLOCK, KV_HEADS, group_size, HEAD_DIM)
    key_rows = got_keys.reshape(span_count, ANC_MAX * BLOCK, KV_HEADS, HEAD_DIM)
    value_rows = got_values.reshape(span_count, ANC_MAX * BLOCK, KV_HEADS, HEAD_DIM)
    scaling = HEAD_DIM ** (-0.5)
    scores = (
        jnp.einsum("rtkgd,rukd->rtkgu", query_rows, key_rows, preferred_element_type=jnp.float32)
        * scaling
    )
    wide_mask = allowed[:, :, None, None, :]
    top_score = jnp.max(jnp.where(wide_mask, scores, -jnp.inf), axis=4)
    weights = jnp.where(wide_mask, jnp.exp(scores - top_score[..., None]), 0.0)
    totals = jnp.sum(weights, axis=4)
    mixed_sum = jnp.einsum(
        "rtkgu,rukd->rtkgd",
        weights.astype(jnp.bfloat16),
        value_rows,
        preferred_element_type=jnp.float32,
    )
    attended = (
        (mixed_sum / totals[..., None]).reshape(tok_rows, HEADS * HEAD_DIM).astype(jnp.bfloat16)
    )
    return attended


def solution(mesh):
    placed = (
        P(("outer", "inner"), None),
        P(("outer", "inner"), None),
        P(("outer", "inner"), None),
        P(),
        P(),
        P(),
    )
    return jax.shard_map(
        shards, mesh=mesh, in_specs=placed, out_specs=P(("outer", "inner"), None), check_vma=False
    )
```

profile of v0, /device:TPU:1, one launch (start us, length us, event | category | flops | bytes accessed | tf_op | source)
XLA Modules:
  0.0 498.6 jit_solution(17158688067835165841)
XLA Ops:
  6.6 1.0 convert_bitcast_fusion.1
  7.7 0.8 fusion.28
  9.2 0.8 copy.67
  10.0 1.1 slice.15
  12.7 1.3 gather_fusion.2
  14.7 55.4 %all-gather.5.cloned.1.call-done = bf16[2048,1024]{1,0:T(8,128)(2,1)} async-done(((bf16[128,1024]{1,0:T(8,128)(2,1)}), bf16[2048,1024]{1,0:T(8,128)(2,1)}) %all-gather.5.cloned.1.call-update) | async-done | bytes 4194320 | tf_op jit(solution)/shard_map/all_gather | solution.py:56
  70.2 7.0 %gather_fusion.7 = bf16[32,128,1024]{2,1,0:T(8,128)(2,1)} fusion(bf16[16,128,1024]{2,1,0:T(8,128)(2,1)} %bitcast.102, s32[1024]{0:T(1024)S(1)} %pad_clamp_fusion.2), kind=kCustom, calls=%fused_computation.7 | custom fusion | bytes 16777344 | tf_op jit(solution)/shard_map/gather | solution.py:75
  77.1 7.8 %all-to-all-start.1 = ((bf16[16,1,2,128,1024]{4,3,2,1,0:T(8,128)(2,1)}), bf16[16,1,2,128,1024]{4,3,2,1,0:T(8,128)(2,1)}, u32[]{:S(2)}, u32[]{:S(2)}) async-start(bf16[16,1,2,128,1024]{4,3,2,1,0:T(8,128)(2,1)} %bitcast.100), calls=%async_computation.1 | async-start | bytes 16777216 | tf_op jit(solution)/shard_map/all_to_all | solution.py:78
  85.7 58.0 %all-gather.3.cloned.1.call-done = bf16[2048,1024]{1,0:T(8,128)(2,1)} async-done(((bf16[128,1024]{1,0:T(8,128)(2,1)}), bf16[2048,1024]{1,0:T(8,128)(2,1)}) %all-gather.3.cloned.1.call-update) | async-done | bytes 4194320 | tf_op jit(solution)/shard_map/all_gather | solution.py:57
  143.7 6.9 %gather_fusion.3 = bf16[32,128,1024]{2,1,0:T(8,128)(2,1)} fusion(bf16[16,128,1024]{2,1,0:T(8,128)(2,1)} %bitcast.103, s32[1024]{0:T(1024)S(1)} %pad_clamp_fusion.2), kind=kCustom, calls=%fused_computation.3 | custom fusion | bytes 16777344 | tf_op jit(solution)/shard_map/gather | solution.py:76
  150.6 117.7 %all-to-all-done.1 = bf16[16,1,2,128,1024]{4,3,2,1,0:T(8,128)(2,1)} async-done(((bf16[16,1,2,128,1024]{4,3,2,1,0:T(8,128)(2,1)}), bf16[16,1,2,128,1024]{4,3,2,1,0:T(8,128)(2,1)}, u32[]{:S(2)}, u32[]{:S(2)}) %all-to-all-start.1) | async-done | bytes 8388640 | tf_op jit(solution)/shard_map/all_to_all | solution.py:78
  268.3 5.7 %all-to-all-start = ((bf16[16,1,2,128,1024]{4,3,2,1,0:T(8,128)(2,1)}), bf16[16,1,2,128,1024]{4,3,2,1,0:T(8,128)(2,1)}, u32[]{:S(2)}, u32[]{:S(2)}) async-start(bf16[16,1,2,128,1024]{4,3,2,1,0:T(8,128)(2,1)} %bitcast.99), calls=%async_computation | async-start | bytes 16777216 | tf_op jit(solution)/shard_map/all_to_all | solution.py:79
  277.5 6.2 %gather_fusion.6 = s32[1024]{0:T(1024)S(1)} fusion(s32[32768]{0:T(1024)S(1)} %copy-done, s32[1024]{0:T(1024)S(1)} %broadcast_clamp_fusion), kind=kCustom, calls=%fused_computation.6 | custom fusion | bytes 12288 | tf_op jit(solution)/shard_map/gather | solution.py:102
  284.7 0.7 fusion.29
  285.4 2.5 subtract_convert_fusion
  288.9 5.5 %gather_fusion.8 = bf16[8,128,1024]{2,1,0:T(8,128)(2,1)} fusion(bf16[32,128,1024]{2,1,0:T(8,128)(2,1)} %bitcast.20, s32[1024]{0:T(1024)S(1)} %pad_clamp_fusion), kind=kCustom, calls=%fused_computation.8 | custom fusion | bytes 4194336 | tf_op jit(solution)/shard_map/gather | solution.py:96
  294.4 2.2 copy.52
  296.6 160.9 %all-to-all-done = bf16[16,1,2,128,1024]{4,3,2,1,0:T(8,128)(2,1)} async-done(((bf16[16,1,2,128,1024]{4,3,2,1,0:T(8,128)(2,1)}), bf16[16,1,2,128,1024]{4,3,2,1,0:T(8,128)(2,1)}, u32[]{:S(2)}, u32[]{:S(2)}) %all-to-all-start) | async-done | bytes 8388640 | tf_op jit(solution)/shard_map/all_to_all | solution.py:79
  457.5 5.4 %gather_fusion.5 = bf16[8,128,1024]{2,1,0:T(8,128)(2,1)} fusion(bf16[32,128,1024]{2,1,0:T(8,128)(2,1)} %bitcast.6, s32[1024]{0:T(1024)S(1)} %pad_clamp_fusion), kind=kCustom, calls=%fused_computation.5 | custom fusion | bytes 4194336 | tf_op jit(solution)/shard_map/gather | solution.py:97
  462.9 3.6 copy.49
  466.5 7.0 %fusion = (f32[128,8,4]{0,2,1:T(4,128)S(1)}, f32[8,1024,128,4]{2,1,3,0:T(8,128)}) fusion(pred[128,1024]{0,1:T(8,128)(4,1)S(1)} %compare_and_fusion, bf16[128,8,4,128]{3,0,2,1:T(8,128)(2,1)S(1)} %bitcast.107, bf16[1024,8,128,1]{2,1,0,3:T(8,128)(2,1)S(1)} %bitcast.104), kind=kOutput, calls=%fused_computation.11 | convolution fusion | flops 1086320640 | bytes 20070400 | tf_op jit(solution)/shard_map/rtkgd,rukd->rtkgu/dot_general | solution.py:112
  473.5 9.3 %fusion.3 = f32[128,8,4]{0,2,1:T(4,128)S(1)} fusion(f32[8,1024,128,4]{2,1,3,0:T(8,128)} %get-tuple-element.42, f32[128,8,4]{0,2,1:T(4,128)S(1)} %get-tuple-element.41, pred[128,1024]{0,1:T(8,128)(4,1)S(1)} %compare_and_fusion), kind=kLoop, calls=%fused_computation.14 | loop fusion | flops 16773120 | bytes 16941056 | tf_op jit(solution)/shard_map/reduce_sum | solution.py:118
  482.8 7.7 %fusion.9 = bf16[1,128,8,4,128]{1,4,3,2,0:T(8,128)(2,1)S(1)} fusion(f32[128,8,4]{0,2,1:T(4,128)S(1)} %fusion.3, f32[8,1024,128,4]{2,1,3,0:T(8,128)} %get-tuple-element.42, f32[128,8,4]{0,2,1:T(4,128)S(1)} %get-tuple-element.41, pred[128,1024]{0,1:T(8,128)(4,1)S(1)} %compare_and_fusion, bf16[1024,8,128,1]{2,1,0,3:T(8,128)(2,1)S(1)} %bitcast.109), kind=kOutput, calls=%fused_computation.20 | convolution fusion | flops 1091567616 | bytes 20086784 | tf_op jit(solution)/shard_map/rtkgu,rukd->rtkgd/dot_general | solution.py:119
  490.4 1.3 copy.39
  (58 shorter events, 7.4 us)
Async XLA Ops:
  6.5 4.6 copy-start.3
  6.5 63.6 %all-gather.5.cloned.1.call-start = ((), (), s32[]{:S(2)}) async-start(), calls=%async_computation.3 | async-start | bytes 4456448 | tf_op jit(solution)/shard_map/all_gather | solution.py:56
  77.1 191.2 %all-to-all-start.1 = ((bf16[16,1,2,128,1024]{4,3,2,1,0:T(8,128)(2,1)}), bf16[16,1,2,128,1024]{4,3,2,1,0:T(8,128)(2,1)}, u32[]{:S(2)}, u32[]{:S(2)}) async-start(bf16[16,1,2,128,1024]{4,3,2,1,0:T(8,128)(2,1)} %bitcast.100), calls=%async_computation.1 | async-start | bytes 16777216 | tf_op jit(solution)/shard_map/all_to_all | solution.py:78
  84.9 58.7 %all-gather.3.cloned.1.call-start = ((), (), s32[]{:S(2)}) async-start(), calls=%async_computation.2 | async-start | bytes 4456448 | tf_op jit(solution)/shard_map/all_gather | solution.py:57
  268.3 9.2 %copy-start = (s32[32768]{0:T(1024)S(1)}, s32[32768]{0:T(1024)}, u32[]{:S(2)}) copy-start(s32[32768]{0:T(1024)} %param.11) | copy-start | bytes 393220
  268.3 189.1 %all-to-all-start = ((bf16[16,1,2,128,1024]{4,3,2,1,0:T(8,128)(2,1)}), bf16[16,1,2,128,1024]{4,3,2,1,0:T(8,128)(2,1)}, u32[]{:S(2)}, u32[]{:S(2)}) async-start(bf16[16,1,2,128,1024]{4,3,2,1,0:T(8,128)(2,1)} %bitcast.99), calls=%async_computation | async-start | bytes 16777216 | tf_op jit(solution)/shard_map/all_to_all | solution.py:79
  274.1 9.6 %copy-start.2 = (bf16[128,4096]{1,0:T(8,128)(2,1)S(1)}, bf16[128,4096]{1,0:T(8,128)(2,1)}, u32[]{:S(2)}) copy-start(bf16[128,4096]{1,0:T(8,128)(2,1)} %param.6) | copy-start | bytes 3145732
  473.5 9.3 %copy-start.1 = (bf16[128,8,8,128]{3,2,1,0:T(8,128)(2,1)S(1)}, bf16[128,8,8,128]{3,2,1,0:T(8,128)(2,1)}, u32[]{:S(2)}) copy-start(bf16[128,8,8,128]{3,2,1,0:T(8,128)(2,1)} %copy.49) | copy-start | bytes 6291460
Sparse Core Ops, SparseCore 0:
  10.1 60.0 all-gather.4
  88.2 55.4 all-gather.2
where the time goes:
time: 499 us
  waiting for transfers between devices  393 us (79%)
  local copies, waits for them, and re-layouts  45.6 us (9%)
  other arithmetic  16.5 us (3%)
  between operations  15.5 us (3%)
  matrix products  14.7 us (3%)
  starting transfers between devices  13.6 us (3%)
    all_to_all x1, waiting for transfers between devices, shards(): lax.all_to_all(send_values, 'outer', split_axis=0, concat_axis=0, tiled=T...  161 us
    all_to_all x1, waiting for transfers between devices, shards(): lax.all_to_all(send_keys, 'outer', split_axis=0, concat_axis=0, tiled=True)  118 us
    all_gather x1, waiting for transfers between devices, shards(): lax.all_gather(values, 'inner', axis=0, tiled=True)  58 us
    all_gather x1, waiting for transfers between devices, shards(): lax.all_gather(rot_k, 'inner', axis=0, tiled=True)  55.4 us
  transfers between devices with their start and end apart: 4, of which 4 were waited for; matrix products, arithmetic and copies ran while one was open for 6% of the time, Pallas kernels for 0%

commit v1 on v0

--- a/solution.py
+++ b/solution.py
@@ -9,6 +9,28 @@
 BLOCK = 128
 ANC_MAX = 8
 ROTARY_BASE = 500000.0
+
+
+def in_order(blocks, dim):
+    dims = list(blocks.shape[1:])
+    dims[dim] *= blocks.shape[0]
+    return jnp.moveaxis(blocks, 0, dim).reshape(dims)
+
+
+def gather_around(value, axis, dim):
+    size = lax.axis_size(axis)
+    pairs = [(i, (i + 1) % size) for i in range(size)]
+    back = [(b, a) for a, b in pairs]
+    lower, upper = ([], [])
+    for step in range(size - 1):
+        if step % 2 == 0:
+            lower.append(lax.ppermute(lower[-1] if lower else value, axis, pairs))
+        else:
+            upper.append(lax.ppermute(upper[-1] if upper else value, axis, back))
+    blocks = jnp.stack([*lower[::-1], value, *upper])
+    shift = lax.axis_index(axis) - len(lower)
+    blocks = blocks[(jnp.arange(size) - shift) % size]
+    return in_order(blocks, dim)
 
 
 def rotate(matrix, places, head_count):
@@ -54,7 +76,7 @@
     slot_ids = jnp.arange(capacity, dtype=jnp.int32)
     bundled = (
         lax.all_gather(rot_k, "inner", axis=0, tiled=True),
-        lax.all_gather(values, "inner", axis=0, tiled=True),
+        gather_around(values, "inner", 0),
     )
     key_blocks = bundled[0].reshape(group_spans, BLOCK, kv_width)
     value_blocks = bundled[1].reshape(group_spans, BLOCK, kv_width)

time: 499 us -> 534 us (1.070)
  starting transfers between devices: 13.6 us -> 58.7 us
  waiting for transfers between devices: 393 us -> 370 us
  local copies, waits for them, and re-layouts: 45.6 us -> 59 us
    all_gather x1 -> x0, waiting for transfers between devices: 58 us -> none  [shards(): lax.all_gather(values, 'inner', axis=0, tiled=True)]
    all_to_all x1, waiting for transfers between devices: 118 us -> 165 us  [shards(): lax.all_to_all(send_keys, 'outer', split_axis=0, concat_axis=0, tiled=True)]
    all_to_all x1, waiting for transfers between devices: 161 us -> 121 us  [shards(): lax.all_to_all(send_values, 'outer', split_axis=0, concat_axis=0, tiled=T...]
    ppermute x0 -> x15, starting transfers between devices: none -> 37.3 us  [the longest x7 35.2 us: gather_around(): upper.append(lax.ppermute(upper[-1] if upper else value, axis, back))]
    ppermute x0 -> x15, waiting for transfers between devices: none -> 30.3 us  [the longest x8 26 us: gather_around(): lower.append(lax.ppermute(lower[-1] if lower else value, axis, pairs))]
    unnamed x14 -> x33, local copies, waits for them, and re-layouts: 7.13 us -> 17.5 us
    all_to_all x1, starting transfers between devices: 5.73 us -> 15.7 us  [shards(): lax.all_to_all(send_values, 'outer', split_axis=0, concat_axis=0, tiled=T...]
  transfers between devices with their start and end apart: 4 -> 18, of which waited for: 4 -> 13; matrix products, arithmetic and copies ran while one was open for 6% -> 9% of each run, Pallas kernels for 0% -> 0%
where the time goes in v1:
time: 534 us
  waiting for transfers between devices  370 us (69%)
  local copies, waits for them, and re-layouts  59 us (11%)
  starting transfers between devices  58.7 us (11%)
  other arithmetic  15.6 us (3%)
  between operations  15.6 us (3%)
  matrix products  14.8 us (3%)
    all_to_all x1, waiting for transfers between devices, shards(): lax.all_to_all(send_keys, 'outer', split_axis=0, concat_axis=0, tiled=True)  165 us
    all_to_all x1, waiting for transfers between devices, shards(): lax.all_to_all(send_values, 'outer', split_axis=0, concat_axis=0, tiled=T...  121 us
    all_gather x1, waiting for transfers between devices, shards(): lax.all_gather(rot_k, 'inner', axis=0, tiled=True)  53.5 us
    ppermute x7, starting transfers between devices, gather_around(): upper.append(lax.ppermute(upper[-1] if upper else value, axis, back))  35.2 us
    ppermute x8, waiting for transfers between devices, gather_around(): lower.append(lax.ppermute(lower[-1] if lower else value, axis, pairs))  26 us
    unnamed x33, local copies, waits for them, and re-layouts  17.5 us
    all_to_all x1, starting transfers between devices, shards(): lax.all_to_all(send_values, 'outer', split_axis=0, concat_axis=0, tiled=T...  15.7 us
  transfers between devices with their start and end apart: 18, of which 13 were waited for; matrix products, arithmetic and copies ran while one was open for 9% of the time, Pallas kernels for 0%

profile of v1, /device:TPU:1, one launch (start us, length us, event | category | flops | bytes accessed | tf_op | source)
XLA Modules:
  0.0 533.5 jit_solution(17651226226439021557)
XLA Ops:
  8.6 8.1 %collective-permute-done = bf16[128,1024]{1,0:T(8,128)(2,1)S(1)} collective-permute-done((bf16[128,1024]{1,0:T(8,128)(2,1)}, bf16[128,1024]{1,0:T(8,128)(2,1)S(1)}, u32[]{:S(2)}, u32[]{:S(2)}) %collective-permute-start) | collective-permute-done | bytes 262176 | tf_op jit(solution)/shard_map/ppermute | solution.py:27
  16.7 4.8 collective-permute-start.8
  26.6 4.8 collective-permute-start.9
  36.3 4.9 collective-permute-start.10
  44.7 5.0 collective-permute-start.11
  53.0 5.2 collective-permute-start.12
  62.5 5.2 collective-permute-start.13
  67.7 3.6 collective-permute-done.6
  73.1 5.2 collective-permute-start.14
  78.4 4.6 collective-permute-done.7
  96.5 5.0 gather_fusion
  101.4 7.0 %gather_fusion.4 = bf16[32,128,1024]{2,1,0:T(8,128)(2,1)} fusion(bf16[16,128,1024]{2,1,0:T(8,128)(2,1)} %gather_fusion, s32[1024]{0:T(1024)S(1)} %pad_clamp_fusion.2), kind=kCustom, calls=%fused_computation.4 | custom fusion | bytes 16777344 | tf_op jit(solution)/shard_map/gather | solution.py:98
  108.4 15.7 %all-to-all-start = ((bf16[16,1,2,128,1024]{4,3,2,1,0:T(8,128)(2,1)}), bf16[16,1,2,128,1024]{4,3,2,1,0:T(8,128)(2,1)}, u32[]{:S(2)}, u32[]{:S(2)}) async-start(bf16[16,1,2,128,1024]{4,3,2,1,0:T(8,128)(2,1)} %bitcast.133), calls=%async_computation | async-start | bytes 16777216 | tf_op jit(solution)/shard_map/all_to_all | solution.py:101
  126.0 53.5 %all-gather.2.cloned.1.call-done = bf16[2048,1024]{1,0:T(8,128)(2,1)} async-done(((bf16[128,1024]{1,0:T(8,128)(2,1)}), bf16[2048,1024]{1,0:T(8,128)(2,1)}) %all-gather.2.cloned.1.call-update) | async-done | bytes 4194320 | tf_op jit(solution)/shard_map/all_gather | solution.py:78
  179.5 7.0 %gather_fusion.8 = bf16[32,128,1024]{2,1,0:T(8,128)(2,1)} fusion(bf16[16,128,1024]{2,1,0:T(8,128)(2,1)} %bitcast.135, s32[1024]{0:T(1024)S(1)} %pad_clamp_fusion.2), kind=kCustom, calls=%fused_computation.8 | custom fusion | bytes 16777344 | tf_op jit(solution)/shard_map/gather | solution.py:97
  186.5 121.0 %all-to-all-done = bf16[16,1,2,128,1024]{4,3,2,1,0:T(8,128)(2,1)} async-done(((bf16[16,1,2,128,1024]{4,3,2,1,0:T(8,128)(2,1)}), bf16[16,1,2,128,1024]{4,3,2,1,0:T(8,128)(2,1)}, u32[]{:S(2)}, u32[]{:S(2)}) %all-to-all-start) | async-done | bytes 8388640 | tf_op jit(solution)/shard_map/all_to_all | solution.py:101
  307.5 5.6 %all-to-all-start.1 = ((bf16[16,1,2,128,1024]{4,3,2,1,0:T(8,128)(2,1)}), bf16[16,1,2,128,1024]{4,3,2,1,0:T(8,128)(2,1)}, u32[]{:S(2)}, u32[]{:S(2)}) async-start(bf16[16,1,2,128,1024]{4,3,2,1,0:T(8,128)(2,1)} %bitcast.132), calls=%async_computation.1 | async-start | bytes 16777216 | tf_op jit(solution)/shard_map/all_to_all | solution.py:100
  313.9 6.2 %gather_fusion.7 = s32[1024]{0:T(1024)S(1)} fusion(s32[32768]{0:T(1024)S(1)} %copy-done, s32[1024]{0:T(1024)S(1)} %broadcast_clamp_fusion), kind=kCustom, calls=%fused_computation.7 | custom fusion | bytes 12288 | tf_op jit(solution)/shard_map/gather | solution.py:124
  325.4 4.1 gather_fusion.6
  331.4 165.1 %all-to-all-done.1 = bf16[16,1,2,128,1024]{4,3,2,1,0:T(8,128)(2,1)} async-done(((bf16[16,1,2,128,1024]{4,3,2,1,0:T(8,128)(2,1)}), bf16[16,1,2,128,1024]{4,3,2,1,0:T(8,128)(2,1)}, u32[]{:S(2)}, u32[]{:S(2)}) %all-to-all-start.1) | async-done | bytes 8388640 | tf_op jit(solution)/shard_map/all_to_all | solution.py:100
  496.5 4.1 gather_fusion.9
  501.2 7.1 %fusion = (f32[128,8,4]{0,2,1:T(4,128)S(1)}, f32[8,1024,128,4]{2,1,3,0:T(8,128)}) fusion(pred[128,1024]{0,1:T(8,128)(4,1)S(1)} %compare_and_fusion, bf16[128,8,4,128]{3,0,2,1:T(8,128)(2,1)S(1)} %bitcast.139, bf16[1024,8,128,1]{2,1,0,3:T(8,128)(2,1)S(1)} %bitcast.136), kind=kOutput, calls=%fused_computation.12 | convolution fusion | flops 1086320640 | bytes 20070400 | tf_op jit(solution)/shard_map/rtkgd,rukd->rtkgu/dot_general | solution.py:134
  508.3 9.4 %fusion.3 = f32[128,8,4]{0,2,1:T(4,128)S(1)} fusion(f32[8,1024,128,4]{2,1,3,0:T(8,128)} %get-tuple-element.42, f32[128,8,4]{0,2,1:T(4,128)S(1)} %get-tuple-element.41, pred[128,1024]{0,1:T(8,128)(4,1)S(1)} %compare_and_fusion), kind=kLoop, calls=%fused_computation.15 | loop fusion | flops 16773120 | bytes 16941056 | tf_op jit(solution)/shard_map/reduce_sum | solution.py:140
  517.7 7.7 %fusion.9 = bf16[1,128,8,4,128]{1,4,3,2,0:T(8,128)(2,1)S(1)} fusion(f32[128,8,4]{0,2,1:T(4,128)S(1)} %fusion.3, f32[8,1024,128,4]{2,1,3,0:T(8,128)} %get-tuple-element.42, f32[128,8,4]{0,2,1:T(4,128)S(1)} %get-tuple-element.41, pred[128,1024]{0,1:T(8,128)(4,1)S(1)} %compare_and_fusion, bf16[1024,8,128,1]{2,1,0,3:T(8,128)(2,1)S(1)} %bitcast.141), kind=kOutput, calls=%fused_computation.21 | convolution fusion | flops 1091567616 | bytes 20086784 | tf_op jit(solution)/shard_map/rtkgu,rukd->rtkgd/dot_general | solution.py:141
  (107 shorter events, 48.2 us)
Async XLA Ops:
  6.5 10.1 %collective-permute-start = (bf16[128,1024]{1,0:T(8,128)(2,1)}, bf16[128,1024]{1,0:T(8,128)(2,1)S(1)}, u32[]{:S(2)}, u32[]{:S(2)}) collective-permute-start(bf16[128,1024]{1,0:T(8,128)(2,1)} %param.8), channel_id=1, source_target_pairs={{0,1},{1,2},{2,3},{3,4},{4,5},{5,6},{6,7},{7,8},{8,9},{9,10},{10,1... | collective-permute-start | bytes 786440 | tf_op jit(solution)/shard_map/ppermute | solution.py:27
  16.7 9.3 %collective-permute-start.1 = (bf16[128,1024]{1,0:T(8,128)(2,1)S(1)}, bf16[128,1024]{1,0:T(8,128)(2,1)S(1)}, u32[]{:S(2)}, u32[]{:S(2)}) collective-permute-start(bf16[128,1024]{1,0:T(8,128)(2,1)S(1)} %collective-permute-done), channel_id=1, source_target_pairs={{0,1},{1,2},{2,3},{3,4},{4,5},{5,6},{6,7},{7,8},{8,9},{9,10},{10,1... | collective-permute-start | bytes 786440 | tf_op jit(solution)/shard_map/ppermute | solution.py:27
  16.7 10.0 %collective-permute-start.8 = (bf16[128,1024]{1,0:T(8,128)(2,1)}, bf16[128,1024]{1,0:T(8,128)(2,1)S(1)}, u32[]{:S(2)}, u32[]{:S(2)}) collective-permute-start(bf16[128,1024]{1,0:T(8,128)(2,1)} %param.8), channel_id=1, source_target_pairs={{1,0},{2,1},{3,2},{4,3},{5,4},{6,5},{7,6},{8,7},{9,8},{10,9},{11,1... | collective-permute-start | bytes 786440 | tf_op jit(solution)/shard_map/ppermute | solution.py:29
  25.9 8.6 %collective-permute-start.2 = (bf16[128,1024]{1,0:T(8,128)(2,1)S(1)}, bf16[128,1024]{1,0:T(8,128)(2,1)S(1)}, u32[]{:S(2)}, u32[]{:S(2)}) collective-permute-start(bf16[128,1024]{1,0:T(8,128)(2,1)S(1)} %collective-permute-done.1), channel_id=1, source_target_pairs={{0,1},{1,2},{2,3},{3,4},{4,5},{5,6},{6,7},{7,8},{8,9},{9,10},{10,1... | collective-permute-start | bytes 786440 | tf_op jit(solution)/shard_map/ppermute | solution.py:27
  26.6 9.6 %collective-permute-start.9 = (bf16[128,1024]{1,0:T(8,128)(2,1)S(1)}, bf16[128,1024]{1,0:T(8,128)(2,1)S(1)}, u32[]{:S(2)}, u32[]{:S(2)}) collective-permute-start(bf16[128,1024]{1,0:T(8,128)(2,1)S(1)} %collective-permute-done.8), channel_id=1, source_target_pairs={{1,0},{2,1},{3,2},{4,3},{5,4},{6,5},{7,6},{8,7},{9,8},{10,9},{11,1... | collective-permute-start | bytes 786440 | tf_op jit(solution)/shard_map/ppermute | solution.py:29
  34.6 8.5 %collective-permute-start.3 = (bf16[128,1024]{1,0:T(8,128)(2,1)S(1)}, bf16[128,1024]{1,0:T(8,128)(2,1)S(1)}, u32[]{:S(2)}, u32[]{:S(2)}) collective-permute-start(bf16[128,1024]{1,0:T(8,128)(2,1)S(1)} %collective-permute-done.2), channel_id=1, source_target_pairs={{0,1},{1,2},{2,3},{3,4},{4,5},{5,6},{6,7},{7,8},{8,9},{9,10},{10,1... | collective-permute-start | bytes 786440 | tf_op jit(solution)/shard_map/ppermute | solution.py:27
  36.3 8.4 %collective-permute-start.10 = (bf16[128,1024]{1,0:T(8,128)(2,1)S(1)}, bf16[128,1024]{1,0:T(8,128)(2,1)S(1)}, u32[]{:S(2)}, u32[]{:S(2)}) collective-permute-start(bf16[128,1024]{1,0:T(8,128)(2,1)S(1)} %collective-permute-done.9), channel_id=1, source_target_pairs={{1,0},{2,1},{3,2},{4,3},{5,4},{6,5},{7,6},{8,7},{9,8},{10,9},{11,1... | collective-permute-start | bytes 786440 | tf_op jit(solution)/shard_map/ppermute | solution.py:29
  43.1 8.5 %collective-permute-start.4 = (bf16[128,1024]{1,0:T(8,128)(2,1)S(1)}, bf16[128,1024]{1,0:T(8,128)(2,1)S(1)}, u32[]{:S(2)}, u32[]{:S(2)}) collective-permute-start(bf16[128,1024]{1,0:T(8,128)(2,1)S(1)} %collective-permute-done.3), channel_id=1, source_target_pairs={{0,1},{1,2},{2,3},{3,4},{4,5},{5,6},{6,7},{7,8},{8,9},{9,10},{10,1... | collective-permute-start | bytes 786440 | tf_op jit(solution)/shard_map/ppermute | solution.py:27
  44.4 46.3 %copy-start.4 = (bf16[128,1024]{1,0:T(8,128)(2,1)S(1)}, bf16[128,1024]{1,0:T(8,128)(2,1)}, u32[]{:S(2)}) copy-start(bf16[128,1024]{1,0:T(8,128)(2,1)} %param.8) | copy-start | bytes 786436
  44.7 8.3 %collective-permute-start.11 = (bf16[128,1024]{1,0:T(8,128)(2,1)S(1)}, bf16[128,1024]{1,0:T(8,128)(2,1)S(1)}, u32[]{:S(2)}, u32[]{:S(2)}) collective-permute-start(bf16[128,1024]{1,0:T(8,128)(2,1)S(1)} %collective-permute-done.10), channel_id=1, source_target_pairs={{1,0},{2,1},{3,2},{4,3},{5,4},{6,5},{7,6},{8,7},{9,8},{10,9},{11,1... | collective-permute-start | bytes 786440 | tf_op jit(solution)/shard_map/ppermute | solution.py:29
  51.6 9.2 %collective-permute-start.5 = (bf16[128,1024]{1,0:T(8,128)(2,1)S(1)}, bf16[128,1024]{1,0:T(8,128)(2,1)S(1)}, u32[]{:S(2)}, u32[]{:S(2)}) collective-permute-start(bf16[128,1024]{1,0:T(8,128)(2,1)S(1)} %collective-permute-done.4), channel_id=1, source_target_pairs={{0,1},{1,2},{2,3},{3,4},{4,5},{5,6},{6,7},{7,8},{8,9},{9,10},{10,1... | collective-permute-start | bytes 786440 | tf_op jit(solution)/shard_map/ppermute | solution.py:27
  53.0 9.5 %collective-permute-start.12 = (bf16[128,1024]{1,0:T(8,128)(2,1)S(1)}, bf16[128,1024]{1,0:T(8,128)(2,1)S(1)}, u32[]{:S(2)}, u32[]{:S(2)}) collective-permute-start(bf16[128,1024]{1,0:T(8,128)(2,1)S(1)} %collective-permute-done.11), channel_id=1, source_target_pairs={{1,0},{2,1},{3,2},{4,3},{5,4},{6,5},{7,6},{8,7},{9,8},{10,9},{11,1... | collective-permute-start | bytes 786440 | tf_op jit(solution)/shard_map/ppermute | solution.py:29
  60.9 10.5 %collective-permute-start.6 = (bf16[128,1024]{1,0:T(8,128)(2,1)S(1)}, bf16[128,1024]{1,0:T(8,128)(2,1)}, u32[]{:S(2)}, u32[]{:S(2)}) collective-permute-start(bf16[128,1024]{1,0:T(8,128)(2,1)S(1)} %collective-permute-done.5), channel_id=1, source_target_pairs={{0,1},{1,2},{2,3},{3,4},{4,5},{5,6},{6,7},{7,8},{8,9},{9,10},{10,1... | collective-permute-start | bytes 786440 | tf_op jit(solution)/shard_map/ppermute | solution.py:27
  62.5 10.6 %collective-permute-start.13 = (bf16[128,1024]{1,0:T(8,128)(2,1)S(1)}, bf16[128,1024]{1,0:T(8,128)(2,1)S(1)}, u32[]{:S(2)}, u32[]{:S(2)}) collective-permute-start(bf16[128,1024]{1,0:T(8,128)(2,1)S(1)} %collective-permute-done.12), channel_id=1, source_target_pairs={{1,0},{2,1},{3,2},{4,3},{5,4},{6,5},{7,6},{8,7},{9,8},{10,9},{11,1... | collective-permute-start | bytes 786440 | tf_op jit(solution)/shard_map/ppermute | solution.py:29
  71.3 11.6 %collective-permute-start.7 = (bf16[128,1024]{1,0:T(8,128)(2,1)}, bf16[128,1024]{1,0:T(8,128)(2,1)}, u32[]{:S(2)}, u32[]{:S(2)}) collective-permute-start(bf16[128,1024]{1,0:T(8,128)(2,1)} %collective-permute-done.6), channel_id=1, source_target_pairs={{0,1},{1,2},{2,3},{3,4},{4,5},{5,6},{6,7},{7,8},{8,9},{9,10},{10,1... | collective-permute-start | bytes 786440 | tf_op jit(solution)/shard_map/ppermute | solution.py:27
  73.1 22.6 %collective-permute-start.14 = (bf16[128,1024]{1,0:T(8,128)(2,1)S(1)}, bf16[128,1024]{1,0:T(8,128)(2,1)S(1)}, u32[]{:S(2)}, u32[]{:S(2)}) collective-permute-start(bf16[128,1024]{1,0:T(8,128)(2,1)S(1)} %collective-permute-done.13), channel_id=1, source_target_pairs={{1,0},{2,1},{3,2},{4,3},{5,4},{6,5},{7,6},{8,7},{9,8},{10,9},{11,1... | collective-permute-start | bytes 786440 | tf_op jit(solution)/shard_map/ppermute | solution.py:29
  108.4 15.8 %copy-start.3 = (bf16[128,1024]{1,0:T(8,128)(2,1)S(1)}, bf16[128,1024]{1,0:T(8,128)(2,1)}, u32[]{:S(2)}) copy-start(bf16[128,1024]{1,0:T(8,128)(2,1)} %param.7) | copy-start | bytes 786436
  108.4 16.0 %copy-start = (s32[32768]{0:T(1024)S(1)}, s32[32768]{0:T(1024)}, u32[]{:S(2)}) copy-start(s32[32768]{0:T(1024)} %param.11) | copy-start | bytes 393220
  108.4 199.1 %all-to-all-start = ((bf16[16,1,2,128,1024]{4,3,2,1,0:T(8,128)(2,1)}), bf16[16,1,2,128,1024]{4,3,2,1,0:T(8,128)(2,1)}, u32[]{:S(2)}, u32[]{:S(2)}) async-start(bf16[16,1,2,128,1024]{4,3,2,1,0:T(8,128)(2,1)} %bitcast.133), calls=%async_computation | async-start | bytes 16777216 | tf_op jit(solution)/shard_map/all_to_all | solution.py:101
  124.1 55.4 %all-gather.2.cloned.1.call-start = ((), (), s32[]{:S(2)}) async-start(), calls=%async_computation.2 | async-start | bytes 4456448 | tf_op jit(solution)/shard_map/all_gather | solution.py:78
  307.5 189.0 %all-to-all-start.1 = ((bf16[16,1,2,128,1024]{4,3,2,1,0:T(8,128)(2,1)}), bf16[16,1,2,128,1024]{4,3,2,1,0:T(8,128)(2,1)}, u32[]{:S(2)}, u32[]{:S(2)}) async-start(bf16[16,1,2,128,1024]{4,3,2,1,0:T(8,128)(2,1)} %bitcast.132), calls=%async_computation.1 | async-start | bytes 16777216 | tf_op jit(solution)/shard_map/all_to_all | solution.py:100
  313.1 6.9 %copy-start.2 = (bf16[128,4096]{1,0:T(8,128)(2,1)S(1)}, bf16[128,4096]{1,0:T(8,128)(2,1)}, u32[]{:S(2)}) copy-start(bf16[128,4096]{1,0:T(8,128)(2,1)} %param.6) | copy-start | bytes 3145732
  320.1 0.7 copy-start.5
  508.3 9.4 %copy-start.1 = (bf16[128,8,8,128]{3,2,1,0:T(8,128)(2,1)S(1)}, bf16[128,8,8,128]{3,2,1,0:T(8,128)(2,1)}, u32[]{:S(2)}) copy-start(bf16[128,8,8,128]{3,2,1,0:T(8,128)(2,1)} %copy.49) | copy-start | bytes 6291460
Sparse Core Ops, SparseCore 0:
  127.4 52.1 all-gather.1
